TPU v7x, 32 devices: a whole 2x2x4 slice. The times are simulated.
32 devices in a mesh: ctx: 16 (over z, y, core), tp: 2 (over x).
Axes of the slice: x: 2, y: 2, z: 4, core: 2. Of those that a mesh axis runs over, the one named last changes fastest.
Arguments:
- activations: bfloat16 [2048, 4096], P(('ctx', 'tp')), may hold values from -24 to 24
- query_weight: bfloat16 [4096, 4096], P(None, 'tp'), may hold values from -0.09375 to 0.09375
- key_weight: bfloat16 [4096, 1024], P(None, 'tp'), may hold values from -0.09375 to 0.09375
- value_weight: bfloat16 [4096, 1024], P(None, 'tp'), may hold values from -0.09375 to 0.09375
Outputs:
- attended: bfloat16 [2048, 4096], P('ctx', 'tp')
All inputs are finite; a program needn't handle non-finite values.
Results may differ from a plain program's by a relative error of at most 0.012.
The roundings to bfloat16 on the way count: a program that leaves them out, or rounds other values in their place, can miss the bound.
Values may be sent and summed in bfloat16 or wider, within the bound.
No kernel may reach another device: no remote copies, remote signals or barrier semaphores. Data moves between devices by JAX's collectives and lax.ppermute only.
A program may use at most 128 MiB of HBM per device.

v0:
```python
import math
import jax
import jax.numpy as jnp
from jax import lax
from jax.sharding import PartitionSpec as P

HD = 128
THETA = 500000.0
NEGATIVE = -1e30


def rotate(heads_in, positions):
    width = heads_in.shape[-1]
    half_width = width // 2
    frequency = THETA ** (-(jnp.arange(half_width).astype(jnp.float32) * 2.0 / width))
    angles = positions[:, None] * frequency[None, :]
    cosine = jnp.cos(angles)[:, None, :]
    sine_table = jnp.sin(angles)[:, None, :]
    front_half = heads_in[..., :half_width]
    back_half = heads_in[..., half_width:]
    return jnp.concatenate(
        [
            front_half * cosine - back_half * sine_table,
            back_half * cosine + front_half * sine_table,
        ],
        axis=-1,
    )


def block_update(state, query_block, query_pos, key_block, value_block, key_pos):
    row_top, totals, accum = state
    scale = 1.0 / math.sqrt(query_block.shape[-1])
    scores = (
        lax.dot_general(
            query_block, key_block, (((1,), (1,)), ((), ())), preferred_element_type=jnp.float32
        )
        * scale
    )
    allowed = key_pos[None, :] <= query_pos[:, None]
    block_top = jnp.max(jnp.where(allowed, scores, NEGATIVE), axis=1)
    new_top = jnp.maximum(row_top, block_top)
    correction = jnp.exp(row_top - new_top)
    weights = jnp.where(allowed, jnp.exp(scores - new_top[:, None]), 0.0)
    totals = totals * correction + jnp.sum(weights, axis=1)
    accum = accum * correction[:, None] + jnp.dot(
        weights.astype(jnp.bfloat16), value_block, preferred_element_type=jnp.float32
    )
    return (new_top, totals, accum)


def attend(groups, keys, values):
    carry_start = []
    for query_rows, query_pos, kv_slot, query_step in groups:
        row_count = query_rows.shape[0]
        blocks_count = row_count // query_step
        carry_start.append(
            (
                jnp.full((blocks_count, query_step), NEGATIVE, jnp.float32),
                jnp.zeros((blocks_count, query_step), jnp.float32),
                jnp.zeros((blocks_count, query_step, HD), jnp.float32),
            )
        )
    carry = tuple(carry_start)
    key_piece = lax.all_gather(keys, "ctx", axis=0, tiled=True)
    value_piece = lax.all_gather(values, "ctx", axis=0, tiled=True)
    piece_rows = key_piece.shape[0]
    key_step = math.gcd(piece_rows, 512)
    updated = []
    for (query_rows, query_pos, kv_slot, query_step), fold_state in zip(groups, carry):
        key_chosen = lax.dynamic_index_in_dim(
            key_piece.reshape(piece_rows, -1, HD), kv_slot, 1, keepdims=False
        )
        value_chosen = lax.dynamic_index_in_dim(
            value_piece.reshape(piece_rows, -1, HD), kv_slot, 1, keepdims=False
        )
        key_blocks = key_chosen.reshape(piece_rows // key_step, key_step, HD)
        value_blocks = value_chosen.reshape(piece_rows // key_step, key_step, HD)
        block_starts = jnp.arange(piece_rows // key_step, dtype=jnp.int32) * key_step
        blocks_count = fold_state[0].shape[0]
        query_blocks = query_rows.reshape(blocks_count, query_step, HD)
        pos_blocks = query_pos.reshape(blocks_count, query_step)

        def per_query(items):
            query_block, pos_block, row_top, totals, accum = items
            last_pos = jnp.max(pos_block)

            def per_key(inner, key_items):
                key_block, value_block, key_start = key_items
                key_pos = key_start + jnp.arange(key_step, dtype=jnp.int32)
                result = lax.cond(
                    key_start <= last_pos,
                    lambda current: block_update(
                        current, query_block, pos_block, key_block, value_block, key_pos
                    ),
                    lambda current: current,
                    inner,
                )
                return (result, None)

            final, unused = lax.scan(
                per_key, (row_top, totals, accum), (key_blocks, value_blocks, block_starts)
            )
            return final

        updated.append(
            lax.map(
                per_query, (query_blocks, pos_blocks, fold_state[0], fold_state[1], fold_state[2])
            )
        )
    final_state = tuple(updated)
    results = []
    for state in final_state:
        outcome = state[2] / state[1][..., None]
        results.append(outcome.reshape(-1, HD))
    return results


def local(activations, query_weight, key_weight, value_weight):
    tensor_count = lax.axis_size("tp")
    context_index = lax.axis_index("ctx")
    local_rows = activations.shape[0] * tensor_count
    heads_here = query_weight.shape[1] // HD
    kv_here = key_weight.shape[1] // HD
    group = heads_here // kv_here
    query_width = heads_here * HD
    key_width = kv_here * HD
    gathered = lax.all_gather(activations, "tp", axis=0, tiled=True)
    projected = jnp.concatenate(
        [
            jnp.dot(gathered, query_weight, preferred_element_type=jnp.float32),
            jnp.dot(gathered, key_weight, preferred_element_type=jnp.float32),
            jnp.dot(gathered, value_weight, preferred_element_type=jnp.float32),
        ],
        axis=1,
    )
    token_pos = context_index * local_rows + jnp.arange(local_rows, dtype=jnp.int32)
    positions = token_pos.astype(jnp.float32)
    queries = rotate(
        projected[:, :query_width].reshape(local_rows, heads_here, HD), positions
    ).astype(jnp.bfloat16)
    keys = (
        rotate(
            projected[:, query_width : query_width + key_width].reshape(local_rows, kv_here, HD),
            positions,
        )
        .astype(jnp.bfloat16)
        .reshape(local_rows, key_width)
    )
    values = projected[:, query_width + key_width :].astype(jnp.bfloat16)
    groups = []
    for kv_slot in range(kv_here):
        chosen = queries[:, kv_slot * group : (kv_slot + 1) * group].reshape(local_rows * group, HD)
        groups.append(
            (chosen, jnp.repeat(token_pos, group), kv_slot, math.gcd(local_rows * group, 512))
        )
    results = attend(groups, keys, values)
    pieces = [outcome.astype(jnp.bfloat16).reshape(local_rows, group * HD) for outcome in results]
    return jnp.concatenate(pieces, axis=1)


def solution(mesh):
    in_specs = (P(("ctx", "tp"), None), P(None, "tp"), P(None, "tp"), P(None, "tp"))
    out_specs = P("ctx", "tp")
    return jax.shard_map(local, mesh=mesh, in_specs=in_specs, out_specs=out_specs, check_vma=False)
```

profile of v0, /device:TPU:25, one launch (start us, length us, event | category | flops | bytes accessed | tf_op | source)
XLA Modules:
  0.0 219.5 jit_solution(12466268835597819170)
XLA Ops:
  7.6 23.6 %all-gather.4.cloned.1.call-done = bf16[128,4096]{1,0:T(8,128)(2,1)} async-done(((bf16[64,4096]{1,0:T(8,128)(2,1)}), bf16[128,4096]{1,0:T(8,128)(2,1)}) %all-gather.4.cloned.1.call-update) | async-done | bytes 1048592 | tf_op jit(solution)/shard_map/all_gather | solution.py:127
  31.2 3.3 %fusion.78 = f32[128,512]{1,0:T(8,128)S(1)} fusion(bf16[128,4096]{1,0:T(8,128)(2,1)} %all-gather.4.cloned.1.call-done, bf16[4096,512]{1,0:T(8,128)(2,1)} %param.22), kind=kOutput, calls=%fused_computation.123 | convolution fusion | flops 536870912 | bytes 5505024 | tf_op jit(solution)/shard_map/dot_general | solution.py:131
  36.0 3.6 %convolution_convert_fusion = bf16[128,512]{1,0:T(8,128)(2,1)} fusion(bf16[128,4096]{1,0:T(8,128)(2,1)S(1)} %copy-done, bf16[4096,512]{1,0:T(8,128)(2,1)} %param.23), kind=kOutput, calls=%fused_computation.93 | convolution fusion | flops 536936448 | bytes 5373952 | tf_op jit(solution)/shard_map/dot_general | solution.py:132
  40.3 8.2 %convolution_bitcast_fusion = f32[16,8,16,128]{3,1,2,0:T(8,128)S(1)} fusion(bf16[128,4096]{1,0:T(8,128)(2,1)S(1)} %copy-done, bf16[4096,2048]{1,0:T(8,128)(2,1)} %param.21), kind=kOutput, calls=%fused_computation.92 | convolution fusion | flops 2147483648 | bytes 18874368 | tf_op jit(solution)/shard_map/dot_general | solution.py:130
  50.6 25.6 %all-gather.6.cloned.1.call-done = bf16[2048,512]{0,1:T(8,128)(2,1)} async-done(((bf16[128,512]{0,1:T(8,128)(2,1)}), bf16[2048,512]{0,1:T(8,128)(2,1)}) %all-gather.6.cloned.1.call-update) | async-done | bytes 2097168 | tf_op jit(solution)/shard_map/all_gather | solution.py:64
  76.1 2.7 %fusion.77 = (bf16[2048,1,128]{0,2,1:T(8,128)(2,1)S(1)}, bf16[2048,1,128]{0,2,1:T(8,128)(2,1)}, bf16[2048,1,128]{0,2,1:T(8,128)(2,1)}, bf16[2048,1,128]{0,2,1:T(8,128)(2,1)}) fusion(bf16[2048,4,128]{0,2,1:T(8,128)(2,1)} %bitcast.80), kind=kLoop, calls=%fused_computation.122 | loop fusion | bytes 4194304 | tf_op jit(solution)/shard_map/jit(dynamic_index_in_dim)/dynamic_slice | solution.py:70
  79.9 39.1 %all-gather.8.cloned.1.call-done = bf16[2048,512]{1,0:T(8,128)(2,1)} async-done(((bf16[128,512]{1,0:T(8,128)(2,1)}), bf16[2048,512]{1,0:T(8,128)(2,1)}) %all-gather.8.cloned.1.call-update) | async-done | bytes 2097168 | tf_op jit(solution)/shard_map/all_gather | solution.py:65
  119.0 2.5 %reshape.177 = bf16[2048,4,128]{2,1,0:T(4,128)(2,1)S(1)} reshape(bf16[2048,512]{1,0:T(8,128)(2,1)} %all-gather.8.cloned.1.call-done) | data formatting | bytes 4194304 | tf_op jit(solution)/shard_map/reshape | solution.py:74
  121.5 4.0 %fusion.76 = (bf16[2048,1,128]{2,1,0:T(2,128)(2,1)S(1)}, bf16[2048,1,128]{2,1,0:T(2,128)(2,1)}, bf16[2048,1,128]{2,1,0:T(2,128)(2,1)}, bf16[2048,1,128]{2,1,0:T(2,128)(2,1)S(1)}) fusion(bf16[2048,4,128]{2,1,0:T(4,128)(2,1)S(1)} %reshape.177), kind=kLoop, calls=%fused_computation.121 | loop fusion | bytes 4194304 | tf_op jit(solution)/shard_map/jit(dynamic_index_in_dim)/dynamic_slice | solution.py:73
  126.5 22.5 %while.96 = (s32[]{:T(128)}, f32[512]{0:T(512)S(1)}, f32[512]{0:T(512)S(1)}, f32[512,128]{1,0:T(8,128)S(1)}, s32[4]{0:T(128)S(1)}, /*index=5*/s32[]{:T(128)}, bf...) while((s32[]{:T(128)}, f32[512]{0:T(512)S(1)}, ...), condition=%wide.region_6.7_spmd.clone, body=%wide.region_1.0_spmd.clone.sunk | while | flops 137496064 | bytes 4122387 | solution.py:100
  128.3 3.8 %conditional.12 = ((f32[512]{0:T(512)S(1)}, f32[512]{0:T(512)S(1)}, f32[512,128]{1,0:T(8,128)S(1)})) conditional(s32[]{:T(128)} %convert_element_type.119, (f32[512]{0:T(512)S(1)}, f32[512]{0:T(512)S(1)}, f32[512,128]{1,0:T(8,128)S(1)}) %tuple.163, (s32[]{:T(128)}, s32[512]{0:T(512)S(1)}, s32[128]{0:T(128)S(1)}, bf16[4,512,128]{2,1,0:T(8,128)(2,1)}, ...), branch_computations={%region_2.2_spmd, %region_3.5_spmd} | conditional | flops 137496064 | bytes 4120100 | solution.py:90
  133.9 3.8 %conditional.12 = ((f32[512]{0:T(512)S(1)}, f32[512]{0:T(512)S(1)}, f32[512,128]{1,0:T(8,128)S(1)})) conditional(s32[]{:T(128)} %convert_element_type.119, (f32[512]{0:T(512)S(1)}, f32[512]{0:T(512)S(1)}, f32[512,128]{1,0:T(8,128)S(1)}) %tuple.163, (s32[]{:T(128)}, s32[512]{0:T(512)S(1)}, s32[128]{0:T(128)S(1)}, bf16[4,512,128]{2,1,0:T(8,128)(2,1)}, ...), branch_computations={%region_2.2_spmd, %region_3.5_spmd} | conditional | flops 137496064 | bytes 4120100 | solution.py:90
  139.5 3.8 %conditional.12 = ((f32[512]{0:T(512)S(1)}, f32[512]{0:T(512)S(1)}, f32[512,128]{1,0:T(8,128)S(1)})) conditional(s32[]{:T(128)} %convert_element_type.119, (f32[512]{0:T(512)S(1)}, f32[512]{0:T(512)S(1)}, f32[512,128]{1,0:T(8,128)S(1)}) %tuple.163, (s32[]{:T(128)}, s32[512]{0:T(512)S(1)}, s32[128]{0:T(128)S(1)}, bf16[4,512,128]{2,1,0:T(8,128)(2,1)}, ...), branch_computations={%region_2.2_spmd, %region_3.5_spmd} | conditional | flops 137496064 | bytes 4120100 | solution.py:90
  145.2 3.8 %conditional.12 = ((f32[512]{0:T(512)S(1)}, f32[512]{0:T(512)S(1)}, f32[512,128]{1,0:T(8,128)S(1)})) conditional(s32[]{:T(128)} %convert_element_type.119, (f32[512]{0:T(512)S(1)}, f32[512]{0:T(512)S(1)}, f32[512,128]{1,0:T(8,128)S(1)}) %tuple.163, (s32[]{:T(128)}, s32[512]{0:T(512)S(1)}, s32[128]{0:T(128)S(1)}, bf16[4,512,128]{2,1,0:T(8,128)(2,1)}, ...), branch_computations={%region_2.2_spmd, %region_3.5_spmd} | conditional | flops 137496064 | bytes 4120100 | solution.py:90
  151.2 23.1 %while.97 = (s32[]{:T(128)}, f32[512]{0:T(512)S(1)}, f32[512]{0:T(512)S(1)}, f32[512,128]{1,0:T(8,128)S(1)}, s32[4]{0:T(128)S(1)}, /*index=5*/s32[]{:T(128)}, bf...) while((s32[]{:T(128)}, f32[512]{0:T(512)S(1)}, ...), condition=%wide.region_12.13_spmd.clone, body=%wide.region_7.12_spmd.clone.sunk | while | flops 137496064 | bytes 4122387 | solution.py:100
  153.1 3.9 %conditional.13 = ((f32[512]{0:T(512)S(1)}, f32[512]{0:T(512)S(1)}, f32[512,128]{1,0:T(8,128)S(1)})) conditional(s32[]{:T(128)} %convert_element_type.120, (f32[512]{0:T(512)S(1)}, f32[512]{0:T(512)S(1)}, f32[512,128]{1,0:T(8,128)S(1)}) %tuple.166, (s32[]{:T(128)}, s32[512]{0:T(512)S(1)}, s32[128]{0:T(128)S(1)}, bf16[4,512,128]{2,1,0:T(8,128)(2,1)}, ...), branch_computations={%region_8.8_spmd, %region_9.11_spmd} | conditional | flops 137496064 | bytes 4120100 | solution.py:90
  155.5 1.4 convolution_add_fusion.1
  158.9 3.9 %conditional.13 = ((f32[512]{0:T(512)S(1)}, f32[512]{0:T(512)S(1)}, f32[512,128]{1,0:T(8,128)S(1)})) conditional(s32[]{:T(128)} %convert_element_type.120, (f32[512]{0:T(512)S(1)}, f32[512]{0:T(512)S(1)}, f32[512,128]{1,0:T(8,128)S(1)}) %tuple.166, (s32[]{:T(128)}, s32[512]{0:T(512)S(1)}, s32[128]{0:T(128)S(1)}, bf16[4,512,128]{2,1,0:T(8,128)(2,1)}, ...), branch_computations={%region_8.8_spmd, %region_9.11_spmd} | conditional | flops 137496064 | bytes 4120100 | solution.py:90
  161.3 1.4 convolution_add_fusion.1
  164.7 3.9 %conditional.13 = ((f32[512]{0:T(512)S(1)}, f32[512]{0:T(512)S(1)}, f32[512,128]{1,0:T(8,128)S(1)})) conditional(s32[]{:T(128)} %convert_element_type.120, (f32[512]{0:T(512)S(1)}, f32[512]{0:T(512)S(1)}, f32[512,128]{1,0:T(8,128)S(1)}) %tuple.166, (s32[]{:T(128)}, s32[512]{0:T(512)S(1)}, s32[128]{0:T(128)S(1)}, bf16[4,512,128]{2,1,0:T(8,128)(2,1)}, ...), branch_computations={%region_8.8_spmd, %region_9.11_spmd} | conditional | flops 137496064 | bytes 4120100 | solution.py:90
  167.1 1.4 convolution_add_fusion.1
  170.4 3.9 %conditional.13 = ((f32[512]{0:T(512)S(1)}, f32[512]{0:T(512)S(1)}, f32[512,128]{1,0:T(8,128)S(1)})) conditional(s32[]{:T(128)} %convert_element_type.120, (f32[512]{0:T(512)S(1)}, f32[512]{0:T(512)S(1)}, f32[512,128]{1,0:T(8,128)S(1)}) %tuple.166, (s32[]{:T(128)}, s32[512]{0:T(512)S(1)}, s32[128]{0:T(128)S(1)}, bf16[4,512,128]{2,1,0:T(8,128)(2,1)}, ...), branch_computations={%region_8.8_spmd, %region_9.11_spmd} | conditional | flops 137496064 | bytes 4120100 | solution.py:90
  175.7 19.9 %while.98 = (s32[]{:T(128)}, f32[512]{0:T(512)S(1)}, f32[512]{0:T(512)S(1)}, f32[512,128]{1,0:T(8,128)S(1)}, s32[4]{0:T(128)S(1)}, /*index=5*/s32[]{:T(128)}, bf...) while((s32[]{:T(128)}, f32[512]{0:T(512)S(1)}, ...), condition=%wide.region_18.19_spmd.clone, body=%wide.region_13.18_spmd.clone.sunk | while | flops 137496064 | bytes 4121879 | solution.py:100
  177.8 2.9 %conditional.14 = ((f32[512]{0:T(512)S(1)}, f32[512]{0:T(512)S(1)}, f32[512,128]{1,0:T(8,128)S(1)})) conditional(s32[]{:T(128)} %convert_element_type.121, (f32[512]{0:T(512)S(1)}, f32[512]{0:T(512)S(1)}, f32[512,128]{1,0:T(8,128)S(1)}) %tuple.169, (s32[]{:T(128)}, s32[512]{0:T(512)S(1)}, s32[128]{0:T(128)S(1)}, bf16[4,512,128]{2,1,0:T(8,128)(2,1)}, ...), branch_computations={%region_14.14_spmd, %region_15.17_spmd} | conditional | flops 137496064 | bytes 4119592 | solution.py:90
  182.7 2.9 %conditional.14 = ((f32[512]{0:T(512)S(1)}, f32[512]{0:T(512)S(1)}, f32[512,128]{1,0:T(8,128)S(1)})) conditional(s32[]{:T(128)} %convert_element_type.121, (f32[512]{0:T(512)S(1)}, f32[512]{0:T(512)S(1)}, f32[512,128]{1,0:T(8,128)S(1)}) %tuple.169, (s32[]{:T(128)}, s32[512]{0:T(512)S(1)}, s32[128]{0:T(128)S(1)}, bf16[4,512,128]{2,1,0:T(8,128)(2,1)}, ...), branch_computations={%region_14.14_spmd, %region_15.17_spmd} | conditional | flops 137496064 | bytes 4119592 | solution.py:90
  187.7 2.9 %conditional.14 = ((f32[512]{0:T(512)S(1)}, f32[512]{0:T(512)S(1)}, f32[512,128]{1,0:T(8,128)S(1)})) conditional(s32[]{:T(128)} %convert_element_type.121, (f32[512]{0:T(512)S(1)}, f32[512]{0:T(512)S(1)}, f32[512,128]{1,0:T(8,128)S(1)}) %tuple.169, (s32[]{:T(128)}, s32[512]{0:T(512)S(1)}, s32[128]{0:T(128)S(1)}, bf16[4,512,128]{2,1,0:T(8,128)(2,1)}, ...), branch_computations={%region_14.14_spmd, %region_15.17_spmd} | conditional | flops 137496064 | bytes 4119592 | solution.py:90
  192.7 2.9 %conditional.14 = ((f32[512]{0:T(512)S(1)}, f32[512]{0:T(512)S(1)}, f32[512,128]{1,0:T(8,128)S(1)})) conditional(s32[]{:T(128)} %convert_element_type.121, (f32[512]{0:T(512)S(1)}, f32[512]{0:T(512)S(1)}, f32[512,128]{1,0:T(8,128)S(1)}) %tuple.169, (s32[]{:T(128)}, s32[512]{0:T(512)S(1)}, s32[128]{0:T(128)S(1)}, bf16[4,512,128]{2,1,0:T(8,128)(2,1)}, ...), branch_computations={%region_14.14_spmd, %region_15.17_spmd} | conditional | flops 137496064 | bytes 4119592 | solution.py:90
  196.3 15.6 %while.99 = (s32[]{:T(128)}, f32[512]{0:T(512)S(1)}, f32[512]{0:T(512)S(1)}, f32[512,128]{1,0:T(8,128)S(1)}, s32[4]{0:T(128)S(1)}, /*index=5*/s32[]{:T(128)}, bf...) while((s32[]{:T(128)}, f32[512]{0:T(512)S(1)}, ...), condition=%wide.region_24.25_spmd.clone, body=%wide.region_19.24_spmd.clone.sunk | while | flops 137496064 | bytes 4121371 | solution.py:100
  198.2 2.0 conditional.15
  202.1 2.0 conditional.15
  206.0 2.0 conditional.15
  209.9 2.0 conditional.15
  (232 shorter events, 67.4 us)
Async XLA Ops:
  6.5 24.7 %all-gather.4.cloned.1.call-start = ((), (), s32[]{:S(2)}) async-start(), calls=%async_computation | async-start | bytes 1572864 | tf_op jit(solution)/shard_map/all_gather | solution.py:127
  7.3 68.9 %all-gather.6.cloned.1.call-start = ((), (), s32[]{:S(2)}) async-start(), calls=%async_computation.1 | async-start | bytes 2228224 | tf_op jit(solution)/shard_map/all_gather | solution.py:64
  31.2 4.8 %copy-start = (bf16[128,4096]{1,0:T(8,128)(2,1)S(1)}, bf16[128,4096]{1,0:T(8,128)(2,1)}, u32[]{:S(2)}) copy-start(bf16[128,4096]{1,0:T(8,128)(2,1)} %all-gather.4.cloned.1.call-done) | copy-start | bytes 3145732
  35.9 83.1 %all-gather.8.cloned.1.call-start = ((), (), s32[]{:S(2)}) async-start(), calls=%async_computation.2 | async-start | bytes 2228224 | tf_op jit(solution)/shard_map/all_gather | solution.py:65
  126.5 22.7 %copy-start.5 = (bf16[2048,1,128]{0,2,1:T(8,128)(2,1)S(1)}, bf16[2048,1,128]{0,2,1:T(8,128)(2,1)}, u32[]{:S(2)}) copy-start(bf16[2048,1,128]{0,2,1:T(8,128)(2,1)} %get-tuple-element.984) | copy-start | bytes 1572868
  126.5 23.7 %copy-start.2 = (bf16[2048,1,128]{2,1,0:T(2,128)(2,1)S(1)}, bf16[2048,1,128]{2,1,0:T(2,128)(2,1)}, u32[]{:S(2)}) copy-start(bf16[2048,1,128]{2,1,0:T(2,128)(2,1)} %get-tuple-element.979) | copy-start | bytes 1572868
  151.2 23.4 %copy-start.4 = (bf16[2048,1,128]{0,2,1:T(8,128)(2,1)S(1)}, bf16[2048,1,128]{0,2,1:T(8,128)(2,1)}, u32[]{:S(2)}) copy-start(bf16[2048,1,128]{0,2,1:T(8,128)(2,1)} %get-tuple-element.983) | copy-start | bytes 1572868
  151.2 24.4 %copy-start.1 = (bf16[2048,1,128]{2,1,0:T(2,128)(2,1)S(1)}, bf16[2048,1,128]{2,1,0:T(2,128)(2,1)}, u32[]{:S(2)}) copy-start(bf16[2048,1,128]{2,1,0:T(2,128)(2,1)} %get-tuple-element.978) | copy-start | bytes 1572868
  175.7 20.1 %copy-start.3 = (bf16[2048,1,128]{0,2,1:T(8,128)(2,1)S(1)}, bf16[2048,1,128]{0,2,1:T(8,128)(2,1)}, u32[]{:S(2)}) copy-start(bf16[2048,1,128]{0,2,1:T(8,128)(2,1)} %get-tuple-element.982) | copy-start | bytes 1572868
Sparse Core Ops, SparseCore 0:
  8.9 22.2 all-gather.3
  36.0 40.0 all-gather.5
  78.3 40.6 all-gather.7
where the time goes:
time: 221 us; the launch traced here: 219 us
  waiting for transfers between devices  89 us (40%)
  matrix products  47.3 us (21%)
  local copies, waits for them, and re-layouts  28.9 us (13%)
  loops' own time  21.6 us (10%)
  other arithmetic  19.1 us (9%)
  between operations  13.5 us (6%)
    all_gather x1, waiting for transfers between devices, attend(): value_piece = lax.all_gather(values, 'ctx', axis=0, tiled=True)  39.1 us
    all_gather x1, waiting for transfers between devices, attend(): key_piece = lax.all_gather(keys, 'ctx', axis=0, tiled=True)  25.6 us
    all_gather x1, waiting for transfers between devices, local(): gathered = lax.all_gather(activations, 'tp', axis=0, tiled=True)  23.6 us
    another operation x4, loops' own time, per_query(): lax.scan(per_key, (row_top, totals, accum), (key_blocks, value_blocks, bl...  20.8 us
    dot_general x16, matrix products, block_update(): lax.dot_general(query_block, key_block, (((1,), (1,)), ((), ())), preferr...  16.5 us
    dot_general x16, matrix products, block_update(): jnp.dot(weights.astype(jnp.bfloat16), value_block, preferred_element_type...  15.7 us
    add x16, other arithmetic, per_key(): key_pos = key_start + jnp.arange(key_step, dtype=jnp.int32)  10.2 us
    dynamic_slice x16, local copies, waits for them, and re-layouts, per_query(): lax.scan(per_key, (row_top, totals, accum), (key_blocks, value_blocks, bl...  9.76 us
  transfers between devices with their start and end apart: 3, of which 3 were waited for; matrix products, arithmetic and copies ran while one was open for 8% of the time, Pallas kernels for 0%

commit v1 on v0

--- a/solution.py
+++ b/solution.py
@@ -7,6 +7,18 @@
 HD = 128
 THETA = 500000.0
 NEGATIVE = -1e30
+
+
+def gather_by_bits(array, axis, dim):
+    ways, here = (lax.axis_size(axis), lax.axis_index(axis))
+    grown, reach = (array, 1)
+    while reach < ways:
+        theirs = lax.ppermute(grown, axis, [(d, d ^ reach) for d in range(ways)])
+        mine_first = jnp.concatenate([grown, theirs], axis=dim)
+        theirs_first = jnp.concatenate([theirs, grown], axis=dim)
+        grown = jnp.where(here & reach == 0, mine_first, theirs_first)
+        reach = 2 * reach
+    return grown
 
 
 def rotate(heads_in, positions):
@@ -61,7 +73,7 @@
             )
         )
     carry = tuple(carry_start)
-    key_piece = lax.all_gather(keys, "ctx", axis=0, tiled=True)
+    key_piece = gather_by_bits(keys, "ctx", 0)
     value_piece = lax.all_gather(values, "ctx", axis=0, tiled=True)
     piece_rows = key_piece.shape[0]
     key_step = math.gcd(piece_rows, 512)

time: 221 us -> 217 us (0.982)
  local copies, waits for them, and re-layouts: 28.9 us -> 24.5 us
  matrix products: 47.3 us -> 44.3 us
  starting transfers between devices: 0.08 us -> 2.43 us
    ppermute x0 -> x4, waiting for transfers between devices: none -> 64.5 us  [gather_by_bits(): theirs = lax.ppermute(grown, axis, [(d, d ^ reach) for d in range(ways)])]
    all_gather x1, waiting for transfers between devices: 39.1 us -> 0.01 us  [attend(): value_piece = lax.all_gather(values, 'ctx', axis=0, tiled=True)]
    all_gather x1 -> x0, waiting for transfers between devices: 25.6 us -> none  [attend(): key_piece = lax.all_gather(keys, 'ctx', axis=0, tiled=True)]
    dot_general x16, matrix products: 15.7 us -> 8.27 us  [block_update(): jnp.dot(weights.astype(jnp.bfloat16), value_block, preferred_element_type...]
    unnamed x21 -> x11, local copies, waits for them, and re-layouts: 5.44 us -> 0.48 us
    reshape x0 -> x1, matrix products: none -> 3.93 us  [local(): projected[:, query_width:query_width + key_width]]
    dot_general x16, matrix products: 16.5 us -> 19.9 us  [block_update(): lax.dot_general(query_block, key_block, (((1,), (1,)), ((), ())), preferr...]
    dot_general x1 -> x0, matrix products: 3.31 us -> none  [local(): jnp.dot(gathered, key_weight, preferred_element_type=jnp.float32)]
  transfers between devices with their start and end apart: 3 -> 6, of which waited for: 3 -> 5; matrix products, arithmetic and copies ran while one was open for 8% -> 10% of each run, Pallas kernels for 0% -> 0%
where the time goes in v1:
time: 217 us; the launch traced here: 216 us
  waiting for transfers between devices  88.9 us (41%)
  matrix products  44.3 us (20%)
  local copies, waits for them, and re-layouts  24.5 us (11%)
  loops' own time  21.2 us (10%)
  other arithmetic  20.4 us (9%)
  between operations  13.8 us (6%)
  starting transfers between devices  2.43 us (1%)
    ppermute x4, waiting for transfers between devices, gather_by_bits(): theirs = lax.ppermute(grown, axis, [(d, d ^ reach) for d in range(ways)])  64.5 us
    all_gather x1, waiting for transfers between devices, local(): gathered = lax.all_gather(activations, 'tp', axis=0, tiled=True)  23.7 us
    another operation x4, loops' own time, per_query(): lax.scan(per_key, (row_top, totals, accum), (key_blocks, value_blocks, bl...  20.5 us
    dot_general x16, matrix products, block_update(): lax.dot_general(query_block, key_block, (((1,), (1,)), ((), ())), preferr...  19.9 us
    add x16, other arithmetic, per_key(): key_pos = key_start + jnp.arange(key_step, dtype=jnp.int32)  10.4 us
    dynamic_slice x16, local copies, waits for them, and re-layouts, per_query(): lax.scan(per_key, (row_top, totals, accum), (key_blocks, value_blocks, bl...  9.49 us
    dot_general x16, matrix products, block_update(): jnp.dot(weights.astype(jnp.bfloat16), value_block, preferred_element_type...  8.27 us
    dot_general x1, matrix products, local(): jnp.dot(gathered, query_weight, preferred_element_type=jnp.float32)  8.22 us
  transfers between devices with their start and end apart: 6, of which 5 were waited for; matrix products, arithmetic and copies ran while one was open for 10% of the time, Pallas kernels for 0%

profile of v1, /device:TPU:25, one launch (start us, length us, event | category | flops | bytes accessed | tf_op | source)
XLA Modules:
  0.0 215.6 jit_solution(2414004716501961658)
XLA Ops:
  7.5 23.7 %all-gather.3.cloned.1.call-done = bf16[128,4096]{1,0:T(8,128)(2,1)} async-done(((bf16[64,4096]{1,0:T(8,128)(2,1)}), bf16[128,4096]{1,0:T(8,128)(2,1)}) %all-gather.3.cloned.1.call-update) | async-done | bytes 1048592 | tf_op jit(solution)/shard_map/all_gather | solution.py:139
  31.2 4.0 %convolution_convert_fusion = bf16[128,512]{1,0:T(8,128)(2,1)} fusion(bf16[128,4096]{1,0:T(8,128)(2,1)} %all-gather.3.cloned.1.call-done, bf16[4096,512]{1,0:T(8,128)(2,1)} %param.23), kind=kOutput, calls=%fused_computation.94 | convolution fusion | flops 536936448 | bytes 5373952 | tf_op jit(solution)/shard_map/dot_general | solution.py:144
  35.2 3.9 %fusion.78 = f32[128,512]{0,1:T(8,128)S(1)} fusion(bf16[128,4096]{1,0:T(8,128)(2,1)S(1)} %copy-done, bf16[4096,512]{1,0:T(8,128)(2,1)} %param.22), kind=kOutput, calls=%fused_computation.130 | convolution fusion | flops 536870912 | bytes 5505024 | tf_op jit(solution)/shard_map/reshape | solution.py:155
  42.3 7.8 %collective-permute-done.1 = bf16[256,512]{0,1:T(8,128)(2,1)S(1)} collective-permute-done((bf16[256,512]{0,1:T(8,128)(2,1)S(1)}, bf16[256,512]{0,1:T(8,128)(2,1)S(1)}, u32[]{:S(2)}, u32[]{:S(2)}) %collective-permute-start.1) | collective-permute-done | bytes 262176 | tf_op jit(solution)/shard_map/ppermute | solution.py:16
  51.5 15.1 %collective-permute-done.2 = bf16[512,512]{0,1:T(8,128)(2,1)S(1)} collective-permute-done((bf16[512,512]{0,1:T(8,128)(2,1)S(1)}, bf16[512,512]{0,1:T(8,128)(2,1)S(1)}, u32[]{:S(2)}, u32[]{:S(2)}) %collective-permute-start.2) | collective-permute-done | bytes 524320 | tf_op jit(solution)/shard_map/ppermute | solution.py:16
  67.0 8.2 %convolution_bitcast_fusion = f32[16,8,16,128]{3,1,2,0:T(8,128)S(1)} fusion(bf16[128,4096]{1,0:T(8,128)(2,1)S(1)} %copy-done, bf16[4096,2048]{1,0:T(8,128)(2,1)} %param.21), kind=kOutput, calls=%fused_computation.93 | convolution fusion | flops 2147483648 | bytes 18874368 | tf_op jit(solution)/shard_map/dot_general | solution.py:142
  77.7 40.5 %collective-permute-done.3 = bf16[1024,512]{0,1:T(8,128)(2,1)S(1)} collective-permute-done((bf16[1024,512]{0,1:T(8,128)(2,1)S(1)}, bf16[1024,512]{0,1:T(8,128)(2,1)S(1)}, u32[]{:S(2)}, u32[]{:S(2)}) %collective-permute-start.3) | collective-permute-done | bytes 1048608 | tf_op jit(solution)/shard_map/ppermute | solution.py:16
  123.3 2.5 %reshape.191 = bf16[2048,4,128]{2,1,0:T(4,128)(2,1)S(1)} reshape(bf16[2048,512]{1,0:T(8,128)(2,1)} %all-gather.5.cloned.1.call-done) | data formatting | bytes 4194304 | tf_op jit(solution)/shard_map/reshape | solution.py:86
  125.8 4.0 %fusion.76 = (bf16[2048,1,128]{2,1,0:T(2,128)(2,1)S(1)}, bf16[2048,1,128]{2,1,0:T(2,128)(2,1)}, bf16[2048,1,128]{2,1,0:T(2,128)(2,1)}, bf16[2048,1,128]{2,1,0:T(2,128)(2,1)S(1)}) fusion(bf16[2048,4,128]{2,1,0:T(4,128)(2,1)S(1)} %reshape.191), kind=kLoop, calls=%fused_computation.128 | loop fusion | bytes 4194304 | tf_op jit(solution)/shard_map/jit(dynamic_index_in_dim)/dynamic_slice | solution.py:85
  130.0 19.3 %while.96 = (s32[]{:T(128)}, f32[512]{0:T(512)S(1)}, f32[512]{0:T(512)S(1)}, f32[512,128]{1,0:T(8,128)S(1)}, s32[4]{0:T(128)S(1)}, /*index=5*/s32[]{:T(128)}, bf...) while((s32[]{:T(128)}, f32[512]{0:T(512)S(1)}, ...), condition=%wide.region_6.7_spmd.clone, body=%wide.region_1.6_spmd.clone.sunk | while | flops 137496064 | bytes 4121879 | solution.py:112
  131.9 2.9 %conditional.12 = ((f32[512]{0:T(512)S(1)}, f32[512]{0:T(512)S(1)}, f32[512,128]{1,0:T(8,128)S(1)})) conditional(s32[]{:T(128)} %convert_element_type.119, (f32[512]{0:T(512)S(1)}, f32[512]{0:T(512)S(1)}, f32[512,128]{1,0:T(8,128)S(1)}) %tuple.154, (s32[]{:T(128)}, s32[512]{0:T(512)S(1)}, s32[128]{0:T(128)S(1)}, bf16[4,512,128]{2,1,0:T(8,128)(2,1)}, ...), branch_computations={%region_2.2_spmd, %region_3.5_spmd} | conditional | flops 137496064 | bytes 4119592 | solution.py:102
  132.7 1.3 fusion.9
  136.7 2.9 %conditional.12 = ((f32[512]{0:T(512)S(1)}, f32[512]{0:T(512)S(1)}, f32[512,128]{1,0:T(8,128)S(1)})) conditional(s32[]{:T(128)} %convert_element_type.119, (f32[512]{0:T(512)S(1)}, f32[512]{0:T(512)S(1)}, f32[512,128]{1,0:T(8,128)S(1)}) %tuple.154, (s32[]{:T(128)}, s32[512]{0:T(512)S(1)}, s32[128]{0:T(128)S(1)}, bf16[4,512,128]{2,1,0:T(8,128)(2,1)}, ...), branch_computations={%region_2.2_spmd, %region_3.5_spmd} | conditional | flops 137496064 | bytes 4119592 | solution.py:102
  137.5 1.3 fusion.9
  141.5 2.9 %conditional.12 = ((f32[512]{0:T(512)S(1)}, f32[512]{0:T(512)S(1)}, f32[512,128]{1,0:T(8,128)S(1)})) conditional(s32[]{:T(128)} %convert_element_type.119, (f32[512]{0:T(512)S(1)}, f32[512]{0:T(512)S(1)}, f32[512,128]{1,0:T(8,128)S(1)}) %tuple.154, (s32[]{:T(128)}, s32[512]{0:T(512)S(1)}, s32[128]{0:T(128)S(1)}, bf16[4,512,128]{2,1,0:T(8,128)(2,1)}, ...), branch_computations={%region_2.2_spmd, %region_3.5_spmd} | conditional | flops 137496064 | bytes 4119592 | solution.py:102
  146.3 2.9 %conditional.12 = ((f32[512]{0:T(512)S(1)}, f32[512]{0:T(512)S(1)}, f32[512,128]{1,0:T(8,128)S(1)})) conditional(s32[]{:T(128)} %convert_element_type.119, (f32[512]{0:T(512)S(1)}, f32[512]{0:T(512)S(1)}, f32[512,128]{1,0:T(8,128)S(1)}) %tuple.154, (s32[]{:T(128)}, s32[512]{0:T(512)S(1)}, s32[128]{0:T(128)S(1)}, bf16[4,512,128]{2,1,0:T(8,128)(2,1)}, ...), branch_computations={%region_2.2_spmd, %region_3.5_spmd} | conditional | flops 137496064 | bytes 4119592 | solution.py:102
  147.2 1.3 fusion.9
  149.7 19.1 %while.97 = (s32[]{:T(128)}, f32[512]{0:T(512)S(1)}, f32[512]{0:T(512)S(1)}, f32[512,128]{1,0:T(8,128)S(1)}, s32[4]{0:T(128)S(1)}, /*index=5*/s32[]{:T(128)}, bf...) while((s32[]{:T(128)}, f32[512]{0:T(512)S(1)}, ...), condition=%wide.region_12.13_spmd.clone, body=%wide.region_7.12_spmd.clone.sunk | while | flops 137496064 | bytes 4121879 | solution.py:112
  151.6 2.9 %conditional.13 = ((f32[512]{0:T(512)S(1)}, f32[512]{0:T(512)S(1)}, f32[512,128]{1,0:T(8,128)S(1)})) conditional(s32[]{:T(128)} %convert_element_type.120, (f32[512]{0:T(512)S(1)}, f32[512]{0:T(512)S(1)}, f32[512,128]{1,0:T(8,128)S(1)}) %tuple.157, (s32[]{:T(128)}, s32[512]{0:T(512)S(1)}, s32[128]{0:T(128)S(1)}, bf16[4,512,128]{2,1,0:T(8,128)(2,1)}, ...), branch_computations={%region_8.8_spmd, %region_9.11_spmd} | conditional | flops 137496064 | bytes 4119592 | solution.py:102
  156.3 2.9 %conditional.13 = ((f32[512]{0:T(512)S(1)}, f32[512]{0:T(512)S(1)}, f32[512,128]{1,0:T(8,128)S(1)})) conditional(s32[]{:T(128)} %convert_element_type.120, (f32[512]{0:T(512)S(1)}, f32[512]{0:T(512)S(1)}, f32[512,128]{1,0:T(8,128)S(1)}) %tuple.157, (s32[]{:T(128)}, s32[512]{0:T(512)S(1)}, s32[128]{0:T(128)S(1)}, bf16[4,512,128]{2,1,0:T(8,128)(2,1)}, ...), branch_computations={%region_8.8_spmd, %region_9.11_spmd} | conditional | flops 137496064 | bytes 4119592 | solution.py:102
  161.1 2.9 %conditional.13 = ((f32[512]{0:T(512)S(1)}, f32[512]{0:T(512)S(1)}, f32[512,128]{1,0:T(8,128)S(1)})) conditional(s32[]{:T(128)} %convert_element_type.120, (f32[512]{0:T(512)S(1)}, f32[512]{0:T(512)S(1)}, f32[512,128]{1,0:T(8,128)S(1)}) %tuple.157, (s32[]{:T(128)}, s32[512]{0:T(512)S(1)}, s32[128]{0:T(128)S(1)}, bf16[4,512,128]{2,1,0:T(8,128)(2,1)}, ...), branch_computations={%region_8.8_spmd, %region_9.11_spmd} | conditional | flops 137496064 | bytes 4119592 | solution.py:102
  165.9 2.9 %conditional.13 = ((f32[512]{0:T(512)S(1)}, f32[512]{0:T(512)S(1)}, f32[512,128]{1,0:T(8,128)S(1)})) conditional(s32[]{:T(128)} %convert_element_type.120, (f32[512]{0:T(512)S(1)}, f32[512]{0:T(512)S(1)}, f32[512,128]{1,0:T(8,128)S(1)}) %tuple.157, (s32[]{:T(128)}, s32[512]{0:T(512)S(1)}, s32[128]{0:T(128)S(1)}, bf16[4,512,128]{2,1,0:T(8,128)(2,1)}, ...), branch_computations={%region_8.8_spmd, %region_9.11_spmd} | conditional | flops 137496064 | bytes 4119592 | solution.py:102
  169.2 19.1 %while.98 = (s32[]{:T(128)}, f32[512]{0:T(512)S(1)}, f32[512]{0:T(512)S(1)}, f32[512,128]{1,0:T(8,128)S(1)}, s32[4]{0:T(128)S(1)}, /*index=5*/s32[]{:T(128)}, bf...) while((s32[]{:T(128)}, f32[512]{0:T(512)S(1)}, ...), condition=%wide.region_18.19_spmd.clone, body=%wide.region_13.18_spmd.clone.sunk | while | flops 137496064 | bytes 4121879 | solution.py:112
  171.0 2.9 %conditional.14 = ((f32[512]{0:T(512)S(1)}, f32[512]{0:T(512)S(1)}, f32[512,128]{1,0:T(8,128)S(1)})) conditional(s32[]{:T(128)} %convert_element_type.121, (f32[512]{0:T(512)S(1)}, f32[512]{0:T(512)S(1)}, f32[512,128]{1,0:T(8,128)S(1)}) %tuple.160, (s32[]{:T(128)}, s32[512]{0:T(512)S(1)}, s32[128]{0:T(128)S(1)}, bf16[4,512,128]{2,1,0:T(8,128)(2,1)}, ...), branch_computations={%region_14.14_spmd, %region_15.17_spmd} | conditional | flops 137496064 | bytes 4119592 | solution.py:102
  175.8 2.9 %conditional.14 = ((f32[512]{0:T(512)S(1)}, f32[512]{0:T(512)S(1)}, f32[512,128]{1,0:T(8,128)S(1)})) conditional(s32[]{:T(128)} %convert_element_type.121, (f32[512]{0:T(512)S(1)}, f32[512]{0:T(512)S(1)}, f32[512,128]{1,0:T(8,128)S(1)}) %tuple.160, (s32[]{:T(128)}, s32[512]{0:T(512)S(1)}, s32[128]{0:T(128)S(1)}, bf16[4,512,128]{2,1,0:T(8,128)(2,1)}, ...), branch_computations={%region_14.14_spmd, %region_15.17_spmd} | conditional | flops 137496064 | bytes 4119592 | solution.py:102
  180.6 2.9 %conditional.14 = ((f32[512]{0:T(512)S(1)}, f32[512]{0:T(512)S(1)}, f32[512,128]{1,0:T(8,128)S(1)})) conditional(s32[]{:T(128)} %convert_element_type.121, (f32[512]{0:T(512)S(1)}, f32[512]{0:T(512)S(1)}, f32[512,128]{1,0:T(8,128)S(1)}) %tuple.160, (s32[]{:T(128)}, s32[512]{0:T(512)S(1)}, s32[128]{0:T(128)S(1)}, bf16[4,512,128]{2,1,0:T(8,128)(2,1)}, ...), branch_computations={%region_14.14_spmd, %region_15.17_spmd} | conditional | flops 137496064 | bytes 4119592 | solution.py:102
  185.3 2.9 %conditional.14 = ((f32[512]{0:T(512)S(1)}, f32[512]{0:T(512)S(1)}, f32[512,128]{1,0:T(8,128)S(1)})) conditional(s32[]{:T(128)} %convert_element_type.121, (f32[512]{0:T(512)S(1)}, f32[512]{0:T(512)S(1)}, f32[512,128]{1,0:T(8,128)S(1)}) %tuple.160, (s32[]{:T(128)}, s32[512]{0:T(512)S(1)}, s32[128]{0:T(128)S(1)}, bf16[4,512,128]{2,1,0:T(8,128)(2,1)}, ...), branch_computations={%region_14.14_spmd, %region_15.17_spmd} | conditional | flops 137496064 | bytes 4119592 | solution.py:102
  188.6 19.1 %while.99 = (s32[]{:T(128)}, f32[512]{0:T(512)S(1)}, f32[512]{0:T(512)S(1)}, f32[512,128]{1,0:T(8,128)S(1)}, s32[4]{0:T(128)S(1)}, /*index=5*/s32[]{:T(128)}, bf...) while((s32[]{:T(128)}, f32[512]{0:T(512)S(1)}, ...), condition=%wide.region_24.25_spmd.clone, body=%wide.region_19.24_spmd.clone.sunk | while | flops 137496064 | bytes 4121879 | solution.py:112
  190.5 2.9 %conditional.15 = ((f32[512]{0:T(512)S(1)}, f32[512]{0:T(512)S(1)}, f32[512,128]{1,0:T(8,128)S(1)})) conditional(s32[]{:T(128)} %convert_element_type.122, (f32[512]{0:T(512)S(1)}, f32[512]{0:T(512)S(1)}, f32[512,128]{1,0:T(8,128)S(1)}) %tuple.163, (s32[]{:T(128)}, s32[512]{0:T(512)S(1)}, s32[128]{0:T(128)S(1)}, bf16[4,512,128]{2,1,0:T(8,128)(2,1)}, ...), branch_computations={%region_20.20_spmd, %region_21.23_spmd} | conditional | flops 137496064 | bytes 4119592 | solution.py:102
  195.2 2.9 %conditional.15 = ((f32[512]{0:T(512)S(1)}, f32[512]{0:T(512)S(1)}, f32[512,128]{1,0:T(8,128)S(1)})) conditional(s32[]{:T(128)} %convert_element_type.122, (f32[512]{0:T(512)S(1)}, f32[512]{0:T(512)S(1)}, f32[512,128]{1,0:T(8,128)S(1)}) %tuple.163, (s32[]{:T(128)}, s32[512]{0:T(512)S(1)}, s32[128]{0:T(128)S(1)}, bf16[4,512,128]{2,1,0:T(8,128)(2,1)}, ...), branch_computations={%region_20.20_spmd, %region_21.23_spmd} | conditional | flops 137496064 | bytes 4119592 | solution.py:102
  200.0 2.9 %conditional.15 = ((f32[512]{0:T(512)S(1)}, f32[512]{0:T(512)S(1)}, f32[512,128]{1,0:T(8,128)S(1)})) conditional(s32[]{:T(128)} %convert_element_type.122, (f32[512]{0:T(512)S(1)}, f32[512]{0:T(512)S(1)}, f32[512,128]{1,0:T(8,128)S(1)}) %tuple.163, (s32[]{:T(128)}, s32[512]{0:T(512)S(1)}, s32[128]{0:T(128)S(1)}, bf16[4,512,128]{2,1,0:T(8,128)(2,1)}, ...), branch_computations={%region_20.20_spmd, %region_21.23_spmd} | conditional | flops 137496064 | bytes 4119592 | solution.py:102
  204.8 2.9 %conditional.15 = ((f32[512]{0:T(512)S(1)}, f32[512]{0:T(512)S(1)}, f32[512,128]{1,0:T(8,128)S(1)})) conditional(s32[]{:T(128)} %convert_element_type.122, (f32[512]{0:T(512)S(1)}, f32[512]{0:T(512)S(1)}, f32[512,128]{1,0:T(8,128)S(1)}) %tuple.163, (s32[]{:T(128)}, s32[512]{0:T(512)S(1)}, s32[128]{0:T(128)S(1)}, bf16[4,512,128]{2,1,0:T(8,128)(2,1)}, ...), branch_computations={%region_20.20_spmd, %region_21.23_spmd} | conditional | flops 137496064 | bytes 4119592 | solution.py:102
  (239 shorter events, 66.8 us)
Async XLA Ops:
  6.5 24.7 %all-gather.3.cloned.1.call-start = ((), (), s32[]{:S(2)}) async-start(), calls=%async_computation | async-start | bytes 1572864 | tf_op jit(solution)/shard_map/all_gather | solution.py:139
  7.3 116.0 %all-gather.5.cloned.1.call-start = ((), (), s32[]{:S(2)}) async-start(), calls=%async_computation.1 | async-start | bytes 2228224 | tf_op jit(solution)/shard_map/all_gather | solution.py:77
  31.2 4.0 %copy-start = (bf16[128,4096]{1,0:T(8,128)(2,1)S(1)}, bf16[128,4096]{1,0:T(8,128)(2,1)}, u32[]{:S(2)}) copy-start(bf16[128,4096]{1,0:T(8,128)(2,1)} %all-gather.3.cloned.1.call-done) | copy-start | bytes 3145732
  39.2 1.7 collective-permute-start
  41.0 9.1 %collective-permute-start.1 = (bf16[256,512]{0,1:T(8,128)(2,1)S(1)}, bf16[256,512]{0,1:T(8,128)(2,1)S(1)}, u32[]{:S(2)}, u32[]{:S(2)}) collective-permute-start(bf16[256,512]{0,1:T(8,128)(2,1)S(1)} %maximum_select_fusion.6), channel_id=1, source_target_pairs={{0,4},{2,6},{4,0},{6,2},{8,12},{10,14},{12,8},{14,10},{16,20},{18,... | collective-permute-start | bytes 786440 | tf_op jit(solution)/shard_map/ppermute | solution.py:16
  50.3 16.3 %collective-permute-start.2 = (bf16[512,512]{0,1:T(8,128)(2,1)S(1)}, bf16[512,512]{0,1:T(8,128)(2,1)S(1)}, u32[]{:S(2)}, u32[]{:S(2)}) collective-permute-start(bf16[512,512]{0,1:T(8,128)(2,1)S(1)} %maximum_select_fusion.4), channel_id=1, source_target_pairs={{0,8},{2,10},{4,12},{6,14},{8,0},{10,2},{12,4},{14,6},{16,24},{18,... | collective-permute-start | bytes 1572872 | tf_op jit(solution)/shard_map/ppermute | solution.py:16
  66.9 51.3 %collective-permute-start.3 = (bf16[1024,512]{0,1:T(8,128)(2,1)S(1)}, bf16[1024,512]{0,1:T(8,128)(2,1)S(1)}, u32[]{:S(2)}, u32[]{:S(2)}) collective-permute-start(bf16[1024,512]{0,1:T(8,128)(2,1)S(1)} %maximum_select_fusion.2), channel_id=1, source_target_pairs={{0,16},{2,18},{4,20},{6,22},{8,24},{10,26},{12,28},{14,30},{16,0},... | collective-permute-start | bytes 3145736 | tf_op jit(solution)/shard_map/ppermute | solution.py:16
  130.0 19.6 %copy-start.2 = (bf16[2048,1,128]{2,1,0:T(2,128)(2,1)S(1)}, bf16[2048,1,128]{2,1,0:T(2,128)(2,1)}, u32[]{:S(2)}) copy-start(bf16[2048,1,128]{2,1,0:T(2,128)(2,1)} %get-tuple-element.899) | copy-start | bytes 1572868
  149.7 19.3 %copy-start.1 = (bf16[2048,1,128]{2,1,0:T(2,128)(2,1)S(1)}, bf16[2048,1,128]{2,1,0:T(2,128)(2,1)}, u32[]{:S(2)}) copy-start(bf16[2048,1,128]{2,1,0:T(2,128)(2,1)} %get-tuple-element.898) | copy-start | bytes 1572868
Sparse Core Ops, SparseCore 0:
  8.9 22.2 all-gather.2
  35.3 64.3 all-gather.4
